TPU v7x, 32 devices: a whole 2x2x4 slice. The times are simulated.
32 devices in a mesh: dp: 8 (over z, core), col: 4 (over y, x).
Axes of the slice: x: 2, y: 2, z: 4, core: 2. Of those that a mesh axis runs over, the one named last changes fastest.
Arguments:
- features: bfloat16 [12288, 256], P(('dp', 'col')), may hold values from -6 to 6
- w_in: bfloat16 [256, 1024], replicated, may hold values from -0.375 to 0.375
- w_out: bfloat16 [1024, 64], replicated, may hold values from -0.1875 to 0.1875
- length_inv: float32 [64], replicated, may hold values from 0.2 to 0.6
- cg_vectors: bfloat16 [12288, 8], P(('dp', 'col')), may hold values from -6 to 6
- cotangent: bfloat16 [12288, 8], P(('dp', 'col')), may hold values from -6 to 6
Outputs:
- product: float32 [12288, 8], P(('dp', 'col'))
- grad_in: float32 [256, 1024], replicated
- grad_out: float32 [1024, 64], replicated
All inputs are finite; a program needn't handle non-finite values.
Results may differ from a plain program's by a relative error of at most 0.03.
Values may be sent and summed in bfloat16 or wider, within the bound.
A program may use at most 64 MiB of HBM per device.

v0:
```python
import math
import jax
import jax.numpy as jnp
from jax import lax
from jax.sharding import PartitionSpec as P


def pair_block(zrow, sqrow, crow, zcol, sqcol, vcol, mixed):
    f32 = jnp.float32
    inner = (((1,), (1,)), ((), ()))
    cross = lax.dot_general(zrow, zcol, inner, preferred_element_type=f32)
    kern = jnp.exp(-0.5 * (sqrow[:, None] + sqcol[None, :] - 2.0 * cross)).astype(jnp.bfloat16)
    prod = jnp.dot(kern, vcol, preferred_element_type=f32)
    pair = lax.dot_general(crow, mixed, inner, preferred_element_type=f32)
    spair = (pair * kern.astype(f32)).astype(jnp.bfloat16)
    acc = jnp.dot(spair, zcol, preferred_element_type=f32)
    rsum = jnp.sum(spair.astype(f32), axis=1)
    return (prod, acc, rsum)


def tile_sums(carry, rows, piece):
    zrow, sqrow, crow = rows
    zcol, vcol, ccol = piece
    width = zrow.shape[1]
    sqcol = jnp.sum(jnp.square(zcol.astype(jnp.float32)), axis=1)
    mixed = jnp.concatenate([vcol, ccol], axis=1)
    count = zcol.shape[0]
    col_block = count if count <= 4096 else math.gcd(count, 4096)
    nrows = zrow.shape[0]
    row_block = math.gcd(nrows, 512)
    row_count = nrows // row_block
    row_parts = (
        zrow.reshape(row_count, row_block, width),
        sqrow.reshape(row_count, row_block),
        crow.reshape(row_count, row_block, crow.shape[1]),
    )

    def step(total, cols):
        zcb, sqcb, vcb, mcb = cols

        def one_rows(block_rows):
            return pair_block(block_rows[0], block_rows[1], block_rows[2], zcb, sqcb, vcb, mcb)

        prod, acc, rsum = lax.map(one_rows, row_parts)
        return (
            (
                total[0] + prod.reshape(nrows, -1),
                total[1] + acc.reshape(nrows, width),
                total[2] + rsum.reshape(nrows),
            ),
            None,
        )

    col_count = count // col_block
    col_parts = (
        zcol.reshape(col_count, col_block, width),
        sqcol.reshape(col_count, col_block),
        vcol.reshape(col_count, col_block, vcol.shape[1]),
        mixed.reshape(col_count, col_block, mixed.shape[1]),
    )
    result, _ = lax.scan(step, carry, col_parts)
    return result


def start_rows(zrow, vrow, crow_in):
    zf = zrow.astype(jnp.float32)
    return (zrow, jnp.sum(zf * zf, axis=1), jnp.concatenate([crow_in, vrow], axis=1))


def empty_sums(nrows, rhs, width):
    return (
        jnp.zeros((nrows, rhs), jnp.float32),
        jnp.zeros((nrows, width), jnp.float32),
        jnp.zeros((nrows,), jnp.float32),
    )


def local(features, w_in, w_out, length_inv, cg_vectors, cotangent):
    f32 = jnp.float32
    pre = jnp.dot(features, w_in, preferred_element_type=f32)
    hidden = jax.nn.silu(pre).astype(jnp.bfloat16)
    embed = jnp.dot(hidden, w_out, preferred_element_type=f32).astype(jnp.bfloat16)
    scaled = (embed.astype(f32) * length_inv).astype(jnp.bfloat16)
    rhs = cg_vectors.shape[1]
    width = scaled.shape[1]
    zrow, vrow, crow_in = (
        lax.all_gather(scaled, "col", axis=0, tiled=True),
        lax.all_gather(cg_vectors, "col", axis=0, tiled=True),
        lax.all_gather(cotangent, "col", axis=0, tiled=True),
    )
    rows = start_rows(zrow, vrow, crow_in)
    prod, acc, rsum = tile_sums(
        empty_sums(zrow.shape[0], rhs, width),
        rows,
        (
            lax.all_gather(scaled, "dp", axis=0, tiled=True),
            lax.all_gather(cg_vectors, "dp", axis=0, tiled=True),
            lax.all_gather(cotangent, "dp", axis=0, tiled=True),
        ),
    )
    partial_grad = acc - rsum[:, None] * zrow.astype(f32)
    product, grad_scaled = (
        lax.psum_scatter(prod.astype(jnp.bfloat16), "col", scatter_dimension=0, tiled=True).astype(
            jnp.float32
        ),
        lax.psum_scatter(
            partial_grad.astype(jnp.bfloat16), "col", scatter_dimension=0, tiled=True
        ).astype(jnp.float32),
    )
    grad_embed = (grad_scaled * length_inv).astype(jnp.bfloat16)
    over_rows = (((0,), (0,)), ((), ()))
    part_out = lax.dot_general(hidden, grad_embed, over_rows, preferred_element_type=f32)
    dhid = lax.dot_general(grad_embed, w_out, (((1,), (1,)), ((), ())), preferred_element_type=f32)
    sig = jax.nn.sigmoid(pre)
    grad_pre = (dhid * sig * (1.0 + pre * (1.0 - sig))).astype(jnp.bfloat16)
    part_in = lax.dot_general(features, grad_pre, over_rows, preferred_element_type=f32)
    grad_in, grad_out = lax.psum((part_in, part_out), ("dp", "col"))
    return (product, grad_in, grad_out)


def solution(mesh):
    placed = (P(("dp", "col"), None), P(), P(), P(), P(("dp", "col"), None), P(("dp", "col"), None))
    return jax.shard_map(
        local,
        mesh=mesh,
        in_specs=placed,
        out_specs=(P(("dp", "col"), None), P(), P()),
        check_vma=False,
    )
```

profile of v0, /device:TPU:0, one launch (start us, length us, event | category | flops | bytes accessed | tf_op | source)
XLA Modules:
  0.0 309.4 jit_solution(6096048379735893209)
XLA Ops:
  7.2 9.9 %all_gather.22 = bf16[1536,8]{0,1:T(8,128)(2,1)S(1)} all-gather(bf16[384,8]{0,1:T(8,128)(2,1)} %param.12), channel_id=1, replica_groups=mesh['dp'=8,'col'=4] {'col'}, dimensions={0}, use_global_device_ids=true | all-gather | bytes 30720 | tf_op jit(solution)/shard_map/all_gather | solution.py:88
  17.1 14.4 %all_gather.20 = bf16[3072,8]{0,1:T(8,128)(2,1)S(1)} all-gather(bf16[384,8]{0,1:T(8,128)(2,1)} %param.12), channel_id=1, replica_groups=mesh['dp'=8,'col'=4] {'dp'}, dimensions={0}, use_global_device_ids=true | all-gather | bytes 55296 | tf_op jit(solution)/shard_map/all_gather | solution.py:97
  31.5 8.0 %all_gather.21 = bf16[1536,8]{0,1:T(8,128)(2,1)S(1)} all-gather(bf16[384,8]{0,1:T(8,128)(2,1)} %param.13), channel_id=1, replica_groups=mesh['dp'=8,'col'=4] {'col'}, dimensions={0}, use_global_device_ids=true | all-gather | bytes 30720 | tf_op jit(solution)/shard_map/all_gather | solution.py:89
  39.5 14.2 %all_gather.23 = bf16[3072,8]{0,1:T(8,128)(2,1)S(1)} all-gather(bf16[384,8]{0,1:T(8,128)(2,1)} %param.13), channel_id=1, replica_groups=mesh['dp'=8,'col'=4] {'dp'}, dimensions={0}, use_global_device_ids=true | all-gather | bytes 55296 | tf_op jit(solution)/shard_map/all_gather | solution.py:98
  53.7 2.6 multiply_convert_fusion.2
  56.7 8.1 %all_gather.18 = bf16[1536,64]{0,1:T(8,128)(2,1)S(1)} all-gather(bf16[384,64]{0,1:T(8,128)(2,1)S(1)} %fusion.9), channel_id=1, replica_groups=mesh['dp'=8,'col'=4] {'col'}, dimensions={0}, use_global_device_ids=true | all-gather | bytes 245760 | tf_op jit(solution)/shard_map/all_gather | solution.py:87
  64.9 14.5 %all_gather.19 = bf16[3072,64]{0,1:T(8,128)(2,1)S(1)} all-gather(bf16[384,64]{0,1:T(8,128)(2,1)S(1)} %fusion.9), channel_id=1, replica_groups=mesh['dp'=8,'col'=4] {'dp'}, dimensions={0}, use_global_device_ids=true | all-gather | bytes 442368 | tf_op jit(solution)/shard_map/all_gather | solution.py:96
  80.9 26.3 %while.25 = (s32[]{:T(128)}, bf16[3,512,8]{1,2,0:T(8,128)(2,1)}, f32[3,512,64]{1,0,2:T(4,128)S(1)}, f32[3,512]{1,0:T(4,128)}, f32[3,512]{1,0:T(4,128)S(1)}, /*in...) while((s32[]{:T(128)}, bf16[3,512,8]{1,2,0:T(8,128)(2,1)}, ...), condition=%wide.region_4.5_spmd, body=%wide.region_2.4_spmd.sunk | while | flops 493878784 | bytes 17899676 | solution.py:44
  80.9 2.3 exponential_convert_fusion.2
  83.2 1.5 fusion.44
  84.7 1.1 convert_reduce_fusion.2
  85.8 1.1 convolution_bitcast_fusion.4
  87.1 1.3 dynamic_update_slice.18
  88.4 1.2 dynamic_update_slice.17
  89.7 2.3 exponential_convert_fusion.2
  92.0 1.5 fusion.44
  93.5 1.1 convert_reduce_fusion.2
  94.6 1.1 convolution_bitcast_fusion.4
  95.9 1.3 dynamic_update_slice.18
  97.2 1.2 dynamic_update_slice.17
  98.4 2.3 exponential_convert_fusion.2
  100.8 1.5 fusion.44
  102.3 1.1 convert_reduce_fusion.2
  104.6 1.3 dynamic_update_slice.18
  106.0 1.2 dynamic_update_slice.17
  109.2 1.7 copy.24
  110.9 23.0 %reduce-scatter.9.cloned.1.call-done = bf16[384,64]{1,0:T(8,128)(2,1)} async-done(((bf16[1536,64]{1,0:T(8,128)(2,1)}), bf16[384,64]{1,0:T(8,128)(2,1)}) %reduce-scatter.9.cloned.1.call-update) | async-done | bytes 49168
  134.9 3.5 %convolution_bitcast_fusion.2 = f32[256,1024]{0,1:T(8,128)} fusion(bf16[384,256]{1,0:T(8,128)(2,1)S(1)} %copy-done.4, f32[384,1024]{1,0:T(8,128)} %get-tuple-element.167, bf16[1024,64]{0,1:T(8,128)(2,1)S(1)} %copy-done.2, bf16[384,64]{0,1:T(8,128)(2,1)S(1)} %copy.27, f32[64]{0:T(128)S(1)} %copy-done.3), kind=kOutput, calls=%fused_computation.16 | convolution fusion | flops 255270912 | bytes 2998528 | tf_op jit(solution)/shard_map/dot_general | solution.py:116
  139.4 21.7 %reduce-scatter.7.cloned.1.call-done = bf16[384,8]{1,0:T(8,128)(2,1)} async-done(((bf16[1536,8]{1,0:T(8,128)(2,1)}), bf16[384,8]{1,0:T(8,128)(2,1)}) %reduce-scatter.7.cloned.1.call-update) | async-done | bytes 6160
  162.7 136.0 %all-reduce.3.cloned.1.call-done = (f32[256,1024]{0,1:T(8,128)}, f32[1024,64]{0,1:T(8,128)}) async-done(((f32[256,1024]{0,1:T(8,128)}, f32[1024,64]{0,1:T(8,128)}), (f32[256,1024]{0,1:T(8,128)}, f32[1024,64]{0,1:T(8,128)})) %all-reduce.3.cloned.1.call-update) | async-done | bytes 1310736 | tf_op jit(solution)/shard_map/psum | solution.py:117
  298.6 2.5 copy.22
  301.2 1.7 copy.55
  (43 shorter events, 8.9 us)
Async XLA Ops:
  7.2 46.6 %copy-start = (bf16[256,1024]{1,0:T(8,128)(2,1)S(1)}, bf16[256,1024]{1,0:T(8,128)(2,1)}, u32[]{:S(2)}) copy-start(bf16[256,1024]{1,0:T(8,128)(2,1)} %param.9) | copy-start | bytes 1572868
  7.2 126.7 %reduce-scatter.9.cloned.1.call-start = ((), (), s32[]{:S(2)}) async-start(), calls=%async_computation.3 | async-start | bytes 491520
  53.7 2.6 copy-start.1
  53.7 2.6 copy-start.3
  107.2 27.6 %copy-start.2 = (bf16[1024,64]{0,1:T(8,128)(2,1)S(1)}, bf16[1024,64]{0,1:T(8,128)(2,1)}, u32[]{:S(2)}) copy-start(bf16[1024,64]{0,1:T(8,128)(2,1)} %param.10) | copy-start | bytes 393220
  107.2 27.6 %copy-start.4 = (bf16[384,256]{1,0:T(8,128)(2,1)S(1)}, bf16[384,256]{1,0:T(8,128)(2,1)}, u32[]{:S(2)}) copy-start(bf16[384,256]{1,0:T(8,128)(2,1)} %param.8) | copy-start | bytes 589828
  109.1 52.0 %reduce-scatter.7.cloned.1.call-start = ((), (), s32[]{:S(2)}) async-start(), calls=%async_computation.2 | async-start | bytes 491520
  110.8 187.8 %all-reduce.3.cloned.1.call-start = ((), (), s32[]{:S(2)}) async-start(), calls=%async_computation.4 | async-start | bytes 2621440 | tf_op jit(solution)/shard_map/psum | solution.py:117
Sparse Core Ops, SparseCore 0:
  109.2 24.5 reduce-scatter.8
  136.6 24.4 reduce-scatter.6
  167.1 131.5 all-reduce.2
where the time goes:
time: 310 us; the launch traced here: 309 us
  waiting for transfers between devices  181 us (58%)
  blocking collectives  69.2 us (22%)
  matrix products  25.6 us (8%)
  local copies, waits for them, and re-layouts  18.3 us (6%)
  between operations  13.9 us (4%)
    psum x1, waiting for transfers between devices, local(): grad_in, grad_out = lax.psum((part_in, part_out), ('dp', 'col'))  136 us
    unnamed x5, waiting for transfers between devices  44.7 us
    all_gather x1, blocking collectives, local(): lax.all_gather(scaled, 'dp', axis=0, tiled=True)  14.5 us
    all_gather x1, blocking collectives, local(): lax.all_gather(cg_vectors, 'dp', axis=0, tiled=True)  14.4 us
    all_gather x1, blocking collectives, local(): lax.all_gather(cotangent, 'dp', axis=0, tiled=True)  14.2 us
    all_gather x1, blocking collectives, local(): lax.all_gather(cg_vectors, 'col', axis=0, tiled=True)  9.88 us
    unnamed x17, local copies, waits for them, and re-layouts  8.87 us
    all_gather x1, blocking collectives, local(): lax.all_gather(scaled, 'col', axis=0, tiled=True)  8.15 us
  transfers between devices with their start and end apart: 3, of which 3 were waited for; matrix products, arithmetic and copies ran while one was open for 3% of the time, Pallas kernels for 0%

commit v1 on v0

--- a/solution.py
+++ b/solution.py
@@ -114,7 +114,7 @@
     sig = jax.nn.sigmoid(pre)
     grad_pre = (dhid * sig * (1.0 + pre * (1.0 - sig))).astype(jnp.bfloat16)
     part_in = lax.dot_general(features, grad_pre, over_rows, preferred_element_type=f32)
-    grad_in, grad_out = lax.psum((part_in, part_out), ("dp", "col"))
+    grad_in, grad_out = lax.psum(lax.psum((part_in, part_out), "col"), "dp")
     return (product, grad_in, grad_out)
 
 

time: 310 us -> 298 us (0.961)
  waiting for transfers between devices: 181 us -> 168 us
    psum x1 -> x2, waiting for transfers between devices: 136 us -> 116 us  [local(): grad_in, grad_out = lax.psum(lax.psum((part_in, part_out), 'col'), 'dp')]
    unnamed x5 -> x6, waiting for transfers between devices: 44.7 us -> 51.9 us
  transfers between devices with their start and end apart: 3 -> 4, of which waited for: 3 -> 4; matrix products, arithmetic and copies ran while one was open for 3% -> 1% of each run, Pallas kernels for 0% -> 0%
where the time goes in v1:
time: 298 us; the launch traced here: 297 us
  waiting for transfers between devices  168 us (56%)
  blocking collectives  69.2 us (23%)
  matrix products  25.6 us (9%)
  local copies, waits for them, and re-layouts  18.3 us (6%)
  between operations  13.9 us (5%)
    psum x2, waiting for transfers between devices, local(): grad_in, grad_out = lax.psum(lax.psum((part_in, part_out), 'col'), 'dp')  116 us
    unnamed x6, waiting for transfers between devices  51.9 us
    all_gather x1, blocking collectives, local(): lax.all_gather(scaled, 'dp', axis=0, tiled=True)  14.5 us
    all_gather x1, blocking collectives, local(): lax.all_gather(cg_vectors, 'dp', axis=0, tiled=True)  14.4 us
    all_gather x1, blocking collectives, local(): lax.all_gather(cotangent, 'dp', axis=0, tiled=True)  14.2 us
    all_gather x1, blocking collectives, local(): lax.all_gather(cg_vectors, 'col', axis=0, tiled=True)  9.88 us
    unnamed x17, local copies, waits for them, and re-layouts  8.87 us
    all_gather x1, blocking collectives, local(): lax.all_gather(scaled, 'col', axis=0, tiled=True)  8.15 us
  transfers between devices with their start and end apart: 4, of which 4 were waited for; matrix products, arithmetic and copies ran while one was open for 1% of the time, Pallas kernels for 0%

profile of v1, /device:TPU:0, one launch (start us, length us, event | category | flops | bytes accessed | tf_op | source)
XLA Modules:
  0.0 296.7 jit_solution(9955718572791926631)
XLA Ops:
  7.2 9.9 %all_gather.22 = bf16[1536,8]{0,1:T(8,128)(2,1)S(1)} all-gather(bf16[384,8]{0,1:T(8,128)(2,1)} %param.12), channel_id=1, replica_groups=mesh['dp'=8,'col'=4] {'col'}, dimensions={0}, use_global_device_ids=true | all-gather | bytes 30720 | tf_op jit(solution)/shard_map/all_gather | solution.py:88
  17.1 14.4 %all_gather.20 = bf16[3072,8]{0,1:T(8,128)(2,1)S(1)} all-gather(bf16[384,8]{0,1:T(8,128)(2,1)} %param.12), channel_id=1, replica_groups=mesh['dp'=8,'col'=4] {'dp'}, dimensions={0}, use_global_device_ids=true | all-gather | bytes 55296 | tf_op jit(solution)/shard_map/all_gather | solution.py:97
  31.5 8.0 %all_gather.21 = bf16[1536,8]{0,1:T(8,128)(2,1)S(1)} all-gather(bf16[384,8]{0,1:T(8,128)(2,1)} %param.13), channel_id=1, replica_groups=mesh['dp'=8,'col'=4] {'col'}, dimensions={0}, use_global_device_ids=true | all-gather | bytes 30720 | tf_op jit(solution)/shard_map/all_gather | solution.py:89
  39.5 14.2 %all_gather.23 = bf16[3072,8]{0,1:T(8,128)(2,1)S(1)} all-gather(bf16[384,8]{0,1:T(8,128)(2,1)} %param.13), channel_id=1, replica_groups=mesh['dp'=8,'col'=4] {'dp'}, dimensions={0}, use_global_device_ids=true | all-gather | bytes 55296 | tf_op jit(solution)/shard_map/all_gather | solution.py:98
  53.7 2.6 multiply_convert_fusion.2
  56.7 8.1 %all_gather.18 = bf16[1536,64]{0,1:T(8,128)(2,1)S(1)} all-gather(bf16[384,64]{0,1:T(8,128)(2,1)S(1)} %fusion.9), channel_id=1, replica_groups=mesh['dp'=8,'col'=4] {'col'}, dimensions={0}, use_global_device_ids=true | all-gather | bytes 245760 | tf_op jit(solution)/shard_map/all_gather | solution.py:87
  64.9 14.5 %all_gather.19 = bf16[3072,64]{0,1:T(8,128)(2,1)S(1)} all-gather(bf16[384,64]{0,1:T(8,128)(2,1)S(1)} %fusion.9), channel_id=1, replica_groups=mesh['dp'=8,'col'=4] {'dp'}, dimensions={0}, use_global_device_ids=true | all-gather | bytes 442368 | tf_op jit(solution)/shard_map/all_gather | solution.py:96
  80.9 26.3 %while.25 = (s32[]{:T(128)}, bf16[3,512,8]{1,2,0:T(8,128)(2,1)}, f32[3,512,64]{1,0,2:T(4,128)S(1)}, f32[3,512]{1,0:T(4,128)}, f32[3,512]{1,0:T(4,128)S(1)}, /*in...) while((s32[]{:T(128)}, bf16[3,512,8]{1,2,0:T(8,128)(2,1)}, ...), condition=%wide.region_4.5_spmd, body=%wide.region_2.4_spmd.sunk | while | flops 493878784 | bytes 17899676 | solution.py:44
  80.9 2.3 exponential_convert_fusion.2
  83.2 1.5 fusion.44
  84.7 1.1 convert_reduce_fusion.2
  87.1 1.3 dynamic_update_slice.18
  88.4 1.2 dynamic_update_slice.17
  89.7 2.3 exponential_convert_fusion.2
  92.0 1.5 fusion.44
  93.5 1.1 convert_reduce_fusion.2
  94.6 1.1 convolution_bitcast_fusion.4
  95.8 1.3 dynamic_update_slice.18
  97.2 1.2 dynamic_update_slice.17
  98.4 2.3 exponential_convert_fusion.2
  100.8 1.5 fusion.44
  102.3 1.1 convert_reduce_fusion.2
  104.6 1.3 dynamic_update_slice.18
  105.9 1.2 dynamic_update_slice.17
  109.2 24.7 %reduce-scatter.9.cloned.1.call-done = bf16[384,64]{1,0:T(8,128)(2,1)} async-done(((bf16[1536,64]{1,0:T(8,128)(2,1)}), bf16[384,64]{1,0:T(8,128)(2,1)}) %reduce-scatter.9.cloned.1.call-update) | async-done | bytes 49168
  135.8 3.5 %convolution_bitcast_fusion.2 = f32[256,1024]{0,1:T(8,128)} fusion(bf16[384,256]{1,0:T(8,128)(2,1)S(1)} %copy-done.4, f32[384,1024]{1,0:T(8,128)} %get-tuple-element.169, bf16[1024,64]{0,1:T(8,128)(2,1)S(1)} %copy-done.2, bf16[384,64]{0,1:T(8,128)(2,1)S(1)} %copy.27, f32[64]{0:T(128)S(1)} %copy-done.3), kind=kOutput, calls=%fused_computation.16 | convolution fusion | flops 255270912 | bytes 2998528 | tf_op jit(solution)/shard_map/dot_general | solution.py:116
  139.4 1.7 copy.24
  141.1 55.1 %all-reduce.7.cloned.1.call-done = (f32[256,1024]{0,1:T(8,128)}, f32[1024,64]{0,1:T(8,128)}) async-done(((f32[256,1024]{0,1:T(8,128)}, f32[1024,64]{0,1:T(8,128)}), (f32[256,1024]{0,1:T(8,128)}, f32[1024,64]{0,1:T(8,128)})) %all-reduce.7.cloned.1.call-update) | async-done | bytes 1310736 | tf_op jit(solution)/shard_map/psum | solution.py:117
  196.2 27.2 %reduce-scatter.7.cloned.1.call-done = bf16[384,8]{1,0:T(8,128)(2,1)} async-done(((bf16[1536,8]{1,0:T(8,128)(2,1)}), bf16[384,8]{1,0:T(8,128)(2,1)}) %reduce-scatter.7.cloned.1.call-update) | async-done | bytes 6160
  225.0 61.0 %all-reduce.5.cloned.1.call-done = (f32[256,1024]{0,1:T(8,128)}, f32[1024,64]{0,1:T(8,128)}) async-done(((f32[256,1024]{0,1:T(8,128)}, f32[1024,64]{0,1:T(8,128)}), (f32[256,1024]{0,1:T(8,128)}, f32[1024,64]{0,1:T(8,128)})) %all-reduce.5.cloned.1.call-update) | async-done | bytes 1310736 | tf_op jit(solution)/shard_map/psum | solution.py:117
  286.0 2.5 copy.22
  288.5 1.7 copy.57
  (46 shorter events, 10.0 us)
Async XLA Ops:
  7.2 46.6 %copy-start = (bf16[256,1024]{1,0:T(8,128)(2,1)S(1)}, bf16[256,1024]{1,0:T(8,128)(2,1)}, u32[]{:S(2)}) copy-start(bf16[256,1024]{1,0:T(8,128)(2,1)} %param.9) | copy-start | bytes 1572868
  7.2 126.6 %reduce-scatter.9.cloned.1.call-start = ((), (), s32[]{:S(2)}) async-start(), calls=%async_computation.3 | async-start | bytes 491520
  53.7 2.6 copy-start.1
  53.7 2.6 copy-start.3
  107.2 28.6 %copy-start.2 = (bf16[1024,64]{0,1:T(8,128)(2,1)S(1)}, bf16[1024,64]{0,1:T(8,128)(2,1)}, u32[]{:S(2)}) copy-start(bf16[1024,64]{0,1:T(8,128)(2,1)} %param.10) | copy-start | bytes 393220
  107.2 28.6 %copy-start.4 = (bf16[384,256]{1,0:T(8,128)(2,1)S(1)}, bf16[384,256]{1,0:T(8,128)(2,1)}, u32[]{:S(2)}) copy-start(bf16[384,256]{1,0:T(8,128)(2,1)} %param.8) | copy-start | bytes 589828
  109.1 87.1 %all-reduce.7.cloned.1.call-start = ((), (), s32[]{:S(2)}) async-start(), calls=%async_computation.5 | async-start | bytes 2621440 | tf_op jit(solution)/shard_map/psum | solution.py:117
  139.3 84.1 %reduce-scatter.7.cloned.1.call-start = ((), (), s32[]{:S(2)}) async-start(), calls=%async_computation.2 | async-start | bytes 491520
  141.0 145.0 %all-reduce.5.cloned.1.call-start = ((), (), s32[]{:S(2)}) async-start(), calls=%async_computation.4 | async-start | bytes 2621440 | tf_op jit(solution)/shard_map/psum | solution.py:117
Sparse Core Ops, SparseCore 0:
  109.2 24.5 reduce-scatter.8
  139.4 56.6 all-reduce.6
  199.0 24.4 reduce-scatter.6
  225.7 60.2 all-reduce.4
